TPU v7x, 512 devices: a whole 4x8x8 slice. The times are simulated.
512 devices in a mesh: dp: 8 (over y), expert: 64 (over x, z, core).
Axes of the slice: x: 4, y: 8, z: 8, core: 2. Of those that a mesh axis runs over, the one named last changes fastest.
Arguments:
- tokens: bfloat16 [8192, 4096], P('expert', 'dp'), may hold values from -6 to 6
- cotangent: bfloat16 [8192, 4096], P('expert', 'dp'), may hold values from -6 to 6
- expert_ids: int32 [8192, 6], P('expert'), may hold values from 0 to 63, all different within a row; in each aligned block of 128 rows (0 to 127, 128 to 255, ...) at most 14 rows name the same one
- route_probs: bfloat16 [8192, 6], P('expert'), may hold values from 0.049804688 to 1
- w_gate: bfloat16 [64, 4096, 768], P('expert', 'dp'), may hold values from -0.09375 to 0.09375
- w_up: bfloat16 [64, 4096, 768], P('expert', 'dp'), may hold values from -0.09375 to 0.09375
- w_down: bfloat16 [64, 768, 4096], P('expert', None, 'dp'), may hold values from -0.09375 to 0.09375
Outputs:
- grad_tokens: bfloat16 [8192, 4096], P('expert', 'dp')
- grad_gate: bfloat16 [64, 4096, 768], P('expert', 'dp')
- grad_up: bfloat16 [64, 4096, 768], P('expert', 'dp')
- grad_down: bfloat16 [64, 768, 4096], P('expert', None, 'dp')
- d_probs: bfloat16 [8192, 6], P('expert')
Inputs may be any that keep to these rules, and one draw needn't show every extreme that they name: `expert_ids`: each row names 6 different experts and every expert is named by some row; in each aligned block of 128 rows no expert is named by more than 14 rows, a bound that some block reaches.
All inputs are finite; a program needn't handle non-finite values.
Results may differ from a plain program's by a relative error of at most 0.024.
Values may be sent and summed in bfloat16 or wider, within the bound.
A program may use at most 64 MiB of HBM per device.

v0:
```python
import jax
import jax.numpy as jnp
from jax import lax
from jax.sharding import PartitionSpec as P


def silu_parts(gate_sum):
    logistic = jax.nn.sigmoid(gate_sum)
    return (gate_sum * logistic, logistic * (1.0 + gate_sum * (1.0 - logistic)))


def local_step(gate_sum, up_sum, grad_h, gate_probs):
    activated, derivative = silu_parts(gate_sum)
    hidden_f = lax.optimization_barrier((activated * up_sum).astype(jnp.bfloat16)).astype(
        jnp.float32
    )
    prob_grad = jnp.sum(hidden_f * grad_h, axis=1).astype(jnp.bfloat16)
    scaled = gate_probs[:, None] * grad_h
    d_gate = (scaled * up_sum * derivative).astype(jnp.bfloat16)
    d_up = (scaled * activated).astype(jnp.bfloat16)
    h_scaled = (gate_probs[:, None] * hidden_f).astype(jnp.bfloat16)
    return (h_scaled, d_gate, d_up, prob_grad)


def contract_rows(a, b):
    return lax.dot_general(a, b, (((0,), (0,)), ((), ())), preferred_element_type=jnp.float32)


def contract_columns(a, b):
    return lax.dot_general(a, b, (((1,), (1,)), ((), ())), preferred_element_type=jnp.float32)


def exchange(rows):
    return lax.all_to_all(rows, "expert", split_axis=0, concat_axis=0, tiled=True)


def local(tokens, cotangent, expert_ids, route_probs, w_gate, w_up, w_down):
    expert_count = lax.axis_size("expert")
    token_count, columns = tokens.shape
    fanout = expert_ids.shape[1]
    capacity = max(2, 7 * token_count * fanout // (6 * expert_count))
    gate_w, up_w, down_w = (w_gate[0], w_up[0], w_down[0])
    experts = jnp.arange(expert_count, dtype=jnp.int32)
    hits = expert_ids.T[:, None, :] == experts[None, :, None]
    chosen = jnp.any(hits, axis=0)
    order = jnp.arange(token_count, dtype=jnp.int32)
    before = (order[:, None] < order[None, :]).astype(jnp.bfloat16)
    earlier = jnp.dot(chosen.astype(jnp.bfloat16), before, preferred_element_type=jnp.float32)
    slot_of = jnp.where(chosen, earlier.astype(jnp.int32), -1)
    probs_f = route_probs.astype(jnp.float32)
    prob_of = jnp.sum(jnp.where(hits, probs_f.T[:, None, :], 0.0), axis=0)
    both = jnp.concatenate([tokens, cotangent], axis=1)
    all_slots = jnp.arange(capacity, dtype=jnp.int32)
    match = slot_of[:, None, :] == all_slots[None, :, None]
    padded = jnp.arange(capacity + 2, dtype=jnp.int32)
    pick = (slot_of[:, None, :] == padded[None, :, None]).astype(jnp.bfloat16)
    rows = (
        jnp.dot(
            pick.reshape(expert_count * (capacity + 2), token_count),
            both,
            preferred_element_type=jnp.float32,
        )
        .astype(jnp.bfloat16)
        .reshape(expert_count, capacity + 2, 2 * columns)
    )
    sent_p = jnp.sum(jnp.where(match, prob_of[:, None, :], 0.0), axis=2).astype(jnp.bfloat16)
    p_row = jnp.pad(sent_p, ((0, 0), (0, 2 * columns - capacity)))
    rows = jnp.where((padded == capacity)[None, :, None], p_row[:, None, :], rows)
    received = exchange(rows)
    rows_all = expert_count * capacity
    gate_probs = received[:, capacity, :capacity].reshape(rows_all).astype(jnp.float32)
    got = received[:, :capacity].reshape(rows_all, 2 * columns)
    x_rows, dy_rows = (got[:, :columns], got[:, columns:])
    parts = (
        jnp.dot(x_rows, gate_w, preferred_element_type=jnp.float32),
        jnp.dot(x_rows, up_w, preferred_element_type=jnp.float32),
        contract_columns(dy_rows, down_w),
    )
    gate_sum, up_sum, grad_h = (
        lax.psum(v.astype(jnp.bfloat16), "dp").astype(jnp.float32) for v in parts
    )
    h_scaled, d_gate, d_up, prob_grad = local_step(gate_sum, up_sum, grad_h, gate_probs)
    dx_rows = contract_columns(d_gate, gate_w) + contract_columns(d_up, up_w)
    dx_rows = dx_rows.astype(jnp.bfloat16).reshape(expert_count, capacity, columns)
    prob_row = jnp.pad(prob_grad.reshape(expert_count, capacity), ((0, 0), (0, columns - capacity)))
    back = exchange(jnp.concatenate([dx_rows, prob_row[:, None, :]], axis=1))
    grad_gate = contract_rows(x_rows, d_gate)
    grad_up = contract_rows(x_rows, d_up)
    grad_down = contract_rows(h_scaled, dy_rows)
    total = contract_rows(
        match.astype(jnp.bfloat16).reshape(rows_all, token_count),
        back[:, :capacity].reshape(rows_all, columns),
    )
    back_p = back[:, capacity, :capacity].astype(jnp.float32)
    back_of = jnp.sum(jnp.where(match, back_p[:, :, None], 0.0), axis=1)
    d_probs = jnp.sum(jnp.where(hits, back_of[None], 0.0), axis=1).T.astype(jnp.bfloat16)
    return (
        total.astype(jnp.bfloat16),
        grad_gate.astype(jnp.bfloat16)[None],
        grad_up.astype(jnp.bfloat16)[None],
        grad_down.astype(jnp.bfloat16)[None],
        d_probs,
    )


def solution(mesh):
    in_specs = (
        P("expert", "dp"),
        P("expert", "dp"),
        P("expert", None),
        P("expert", None),
        P("expert", "dp", None),
        P("expert", "dp", None),
        P("expert", None, "dp"),
    )
    out_specs = (
        P("expert", "dp"),
        P("expert", "dp", None),
        P("expert", "dp", None),
        P("expert", None, "dp"),
        P("expert", None),
    )
    return jax.shard_map(local, mesh=mesh, in_specs=in_specs, out_specs=out_specs, check_vma=False)
```

profile of v0, /device:TPU:1, one launch (start us, length us, event | category | flops | bytes accessed | tf_op | source)
XLA Modules:
  0.0 261.2 jit_solution(15965414682091480196)
XLA Ops:
  7.2 0.7 convert_bitcast_fusion
  8.8 0.7 select_reduce_fusion.3
  10.2 1.7 convolution_convert_fusion
  12.1 65.8 %all_to_all.10 = bf16[64,16,1024]{2,1,0:T(8,128)(2,1)S(1)} all-to-all(bf16[64,16,1024]{2,1,0:T(8,128)(2,1)S(1)} %broadcast_select_fusion), channel_id=1, replica_groups=mesh['dp'=8,'expert'=64] {'expert'}, dimensions={0} | all-to-all | bytes 4194304 | tf_op jit(solution)/shard_map/all_to_all | solution.py:34
  78.0 1.5 reshape.52
  79.5 3.4 %convolution_convert_fusion.1 = bf16[896,768]{1,0:T(8,128)(2,1)} fusion(bf16[1,512,768]{2,1,0:T(8,128)(2,1)S(1)} %copy-done, bf16[896,1024]{1,0:T(8,128)(2,1)} %reshape.52), kind=kOutput, calls=%fused_computation.23 | convolution fusion | flops 705331200 | bytes 3080192 | tf_op jit(solution)/shard_map/dot_general | solution.py:75
  82.9 2.0 convolution_convert_fusion.2
  84.9 2.0 convolution_convert_fusion.3
  87.2 109.1 %all-reduce.5.cloned.1.call-done = (bf16[896,768]{1,0:T(8,128)(2,1)}, bf16[896,768]{1,0:T(8,128)(2,1)}, bf16[896,768]{1,0:T(8,128)(2,1)}) async-done(((bf16[896,768]{1,0:T(8,128)(2,1)}, bf16[896,768]{1,0:T(8,128)(2,1)}, bf16[896,768]{1,0:T(8,128)(2,1)}), (bf16[896,768]{1,0:T(8,128)(2,1)}, bf16[896,768]{1,0:T(8,128)(2,1)}, bf16[896,768]{1,0:T(8,128)(2,1)})) %all-reduce.5.cloned.1.call-update) | async-done | bytes 4128784 | tf_op jit(solution)/shard_map/psum | solution.py:80
  196.3 4.5 %fusion.1 = (bf16[896,768]{1,0:T(8,128)(2,1)}, bf16[896,768]{1,0:T(8,128)(2,1)S(1)}, bf16[896,768]{1,0:T(8,128)(2,1)S(1)}) fusion(bf16[896,768]{1,0:T(8,128)(2,1)} %get-tuple-element.5, f32[896]{0:T(1024)S(1)} %reshape.54, bf16[896,768]{1,0:T(8,128)(2,1)} %get-tuple-element.7, bf16[896,768]{1,0:T(8,128)(2,1)} %get-tuple-element.6), kind=kLoop, calls=%fused_computation.9 | loop fusion | flops 13074432 | bytes 8261120 | tf_op jit(solution)/shard_map/convert_element_type | solution.py:20
  200.8 1.0 fusion.5
  201.8 0.8 convert_element_type.116
  202.7 0.8 copy.24
  203.4 0.9 fusion.24
  205.0 1.8 add_convert_fusion
  206.8 1.4 reshape.53
  208.2 1.3 pad_maximum_fusion
  209.5 11.5 %all-to-all-start.1 = ((bf16[64,15,512]{2,1,0:T(8,128)(2,1)}), bf16[64,15,512]{2,1,0:T(8,128)(2,1)}, u32[]{:S(2)}, u32[]{:S(2)}) async-start(bf16[64,15,512]{2,1,0:T(8,128)(2,1)} %pad_maximum_fusion), calls=%async_computation.1 | async-start | bytes 2097152 | tf_op jit(solution)/shard_map/all_to_all | solution.py:34
  221.1 3.2 %fusion.15 = bf16[1,512,768]{2,1,0:T(8,128)(2,1)} fusion(bf16[896,768]{1,0:T(8,128)(2,1)S(1)} %copy-done.7, bf16[896,1024]{1,0:T(8,128)(2,1)} %reshape.52), kind=kOutput, calls=%fused_computation.31 | convolution fusion | flops 705036288 | bytes 3080192 | tf_op jit(solution)/shard_map/dot_general | solution.py:26
  224.3 1.9 fusion.14
  226.3 2.0 fusion.16
  228.3 21.2 %all-to-all-done.1 = bf16[64,15,512]{2,1,0:T(8,128)(2,1)} async-done(((bf16[64,15,512]{2,1,0:T(8,128)(2,1)}), bf16[64,15,512]{2,1,0:T(8,128)(2,1)}, u32[]{:S(2)}, u32[]{:S(2)}) %all-to-all-start.1) | async-done | bytes 983072 | tf_op jit(solution)/shard_map/all_to_all | solution.py:34
  249.5 0.9 slice_convert_fusion
  250.7 3.0 %fusion.19 = bf16[128,512]{1,0:T(8,128)(2,1)} fusion(bf16[64,14,512]{2,1,0:T(8,128)(2,1)} %bitcast.42, s32[64,128]{1,0:T(8,128)S(1)} %copy-done.10), kind=kOutput, calls=%fused_computation.34 | convolution fusion | flops 117620736 | bytes 1081344 | tf_op jit(solution)/shard_map/dot_general | solution.py:26
  (52 shorter events, 3.6 us)
Async XLA Ops:
  7.2 72.3 %copy-start = (bf16[1,512,768]{2,1,0:T(8,128)(2,1)S(1)}, bf16[1,512,768]{2,1,0:T(8,128)(2,1)}, u32[]{:S(2)}) copy-start(bf16[1,512,768]{2,1,0:T(8,128)(2,1)} %param.11) | copy-start | bytes 2359300
  7.2 189.1 %all-reduce.5.cloned.1.call-start = ((), (), s32[]{:S(2)}) async-start(), calls=%async_computation.2 | async-start | bytes 8257536 | tf_op jit(solution)/shard_map/psum | solution.py:80
  8.8 3.0 %copy-start.9 = (s32[64,128]{1,0:T(8,128)}, s32[64,128]{1,0:T(8,128)S(1)}, u32[]{:S(2)}) copy-start(s32[64,128]{1,0:T(8,128)S(1)} %fusion.20) | copy-start | bytes 98308
  79.5 3.4 %copy-start.2 = (bf16[896,1024]{1,0:T(8,128)(2,1)S(1)}, bf16[896,1024]{1,0:T(8,128)(2,1)}, u32[]{:S(2)}) copy-start(bf16[896,1024]{1,0:T(8,128)(2,1)} %reshape.52) | copy-start | bytes 5505028
  79.5 3.4 %copy-start.15 = (bf16[1,512,768]{2,1,0:T(8,128)(2,1)S(1)}, bf16[1,512,768]{2,1,0:T(8,128)(2,1)}, u32[]{:S(2)}) copy-start(bf16[1,512,768]{2,1,0:T(8,128)(2,1)} %param.12) | copy-start | bytes 2359300
  82.9 2.0 copy-start.14
  87.2 113.6 %copy-start.12 = (f32[896]{0:T(1024)}, f32[896]{0:T(1024)S(1)}, u32[]{:S(2)}) copy-start(f32[896]{0:T(1024)S(1)} %reshape.54) | copy-start | bytes 10756
  196.3 4.5 %copy-start.1 = (bf16[896,768]{1,0:T(8,128)(2,1)S(1)}, bf16[896,768]{1,0:T(8,128)(2,1)}, u32[]{:S(2)}) copy-start(bf16[896,768]{1,0:T(8,128)(2,1)} %get-tuple-element.5) | copy-start | bytes 4128772
  200.8 3.5 %copy-start.4 = (bf16[896,768]{1,0:T(8,128)(2,1)}, bf16[896,768]{1,0:T(8,128)(2,1)S(1)}, u32[]{:S(2)}) copy-start(bf16[896,768]{1,0:T(8,128)(2,1)S(1)} %get-tuple-element.9) | copy-start | bytes 4128772
  203.4 1.3 copy-start.6
  203.4 1.5 copy-start.16
  206.8 1.4 copy-start.8
  209.5 11.5 %copy-start.7 = (bf16[896,768]{1,0:T(8,128)(2,1)S(1)}, bf16[896,768]{1,0:T(8,128)(2,1)}, u32[]{:S(2)}) copy-start(bf16[896,768]{1,0:T(8,128)(2,1)} %get-tuple-element.8) | copy-start | bytes 4128772
  209.5 40.0 %all-to-all-start.1 = ((bf16[64,15,512]{2,1,0:T(8,128)(2,1)}), bf16[64,15,512]{2,1,0:T(8,128)(2,1)}, u32[]{:S(2)}, u32[]{:S(2)}) async-start(bf16[64,15,512]{2,1,0:T(8,128)(2,1)} %pad_maximum_fusion), calls=%async_computation.1 | async-start | bytes 2097152 | tf_op jit(solution)/shard_map/all_to_all | solution.py:34
  221.1 3.3 %copy-start.3 = (bf16[896,1024]{1,0:T(8,128)(2,1)S(1)}, bf16[896,1024]{1,0:T(8,128)(2,1)}, u32[]{:S(2)}) copy-start(bf16[896,1024]{1,0:T(8,128)(2,1)} %reshape.52) | copy-start | bytes 5505028
  221.1 3.3 %copy-start.5 = (bf16[896,768]{1,0:T(8,128)(2,1)S(1)}, bf16[896,768]{1,0:T(8,128)(2,1)}, u32[]{:S(2)}) copy-start(bf16[896,768]{1,0:T(8,128)(2,1)} %copy-done.4) | copy-start | bytes 4128772
  224.3 1.9 copy-start.13
  226.3 24.2 %copy-start.10 = (s32[64,128]{1,0:T(8,128)S(1)}, s32[64,128]{1,0:T(8,128)}, u32[]{:S(2)}) copy-start(s32[64,128]{1,0:T(8,128)} %copy-done.9) | copy-start | bytes 98308
  226.3 27.5 %copy-start.11 = (s32[128,6]{0,1:T(8,128)S(1)}, s32[128,6]{0,1:T(8,128)}, u32[]{:S(2)}) copy-start(s32[128,6]{0,1:T(8,128)} %param.9) | copy-start | bytes 9220
Sparse Core Ops, SparseCore 0:
  87.0 109.2 all-reduce.4
where the time goes:
time: 262 us; the launch traced here: 261 us
  waiting for transfers between devices  130 us (50%)
  blocking collectives  65.8 us (25%)
  matrix products  22.1 us (8%)
  between operations  14.2 us (5%)
  starting transfers between devices  11.6 us (4%)
  other arithmetic  11.5 us (4%)
  local copies, waits for them, and re-layouts  5.61 us (2%)
    psum x1, waiting for transfers between devices, local(): lax.psum(v.astype(jnp.bfloat16), 'dp').astype(jnp.float32)  109 us
    all_to_all x1, blocking collectives, exchange(): lax.all_to_all(rows, 'expert', split_axis=0, concat_axis=0, tiled=True)  65.8 us
    all_to_all x1, waiting for transfers between devices, exchange(): lax.all_to_all(rows, 'expert', split_axis=0, concat_axis=0, tiled=True)  21.2 us
    all_to_all x1, starting transfers between devices, exchange(): lax.all_to_all(rows, 'expert', split_axis=0, concat_axis=0, tiled=True)  11.5 us
    dot_general x4, matrix products, contract_rows(): lax.dot_general(a, b, (((0,), (0,)), ((), ())), preferred_element_type=jn...  10.2 us
  transfers between devices with their start and end apart: 2, of which 2 were waited for; matrix products, arithmetic and copies ran while one was open for 3% of the time, Pallas kernels for 0%

commit v1 on v0

--- a/solution.py
+++ b/solution.py
@@ -2,6 +2,7 @@
 import jax.numpy as jnp
 from jax import lax
 from jax.sharding import PartitionSpec as P
+from jax.lax import all_gather
 
 
 def silu_parts(gate_sum):
@@ -77,7 +78,8 @@
         contract_columns(dy_rows, down_w),
     )
     gate_sum, up_sum, grad_h = (
-        lax.psum(v.astype(jnp.bfloat16), "dp").astype(jnp.float32) for v in parts
+        all_gather(v.astype(jnp.bfloat16), axis_name="dp").sum(axis=0).astype(jnp.float32)
+        for v in parts
     )
     h_scaled, d_gate, d_up, prob_grad = local_step(gate_sum, up_sum, grad_h, gate_probs)
     dx_rows = contract_columns(d_gate, gate_w) + contract_columns(d_up, up_w)

time: 262 us -> 513 us (1.96)
  waiting for transfers between devices: 130 us -> 362 us
  other arithmetic: 11.5 us -> 31 us
    all_gather x0 -> x3, waiting for transfers between devices: none -> 341 us  [local(): all_gather(v.astype(jnp.bfloat16), axis_name='dp').sum(axis=0)]
    psum x1 -> x0, waiting for transfers between devices: 109 us -> none  [local(): lax.psum(v.astype(jnp.bfloat16), 'dp').astype(jnp.float32)]
    reduce_sum x0 -> x3, other arithmetic: none -> 20.2 us  [local(): all_gather(v.astype(jnp.bfloat16), axis_name='dp').sum(axis=0)]
  transfers between devices with their start and end apart: 2 -> 4, of which waited for: 2 -> 4; matrix products, arithmetic and copies ran while one was open for 3% -> 5% of each run, Pallas kernels for 0% -> 0%
where the time goes in v1:
time: 513 us; the launch traced here: 512 us
  waiting for transfers between devices  362 us (71%)
  blocking collectives  65.8 us (13%)
  other arithmetic  31 us (6%)
  matrix products  23.9 us (5%)
  between operations  13.9 us (3%)
  starting transfers between devices  11.8 us (2%)
    all_gather x3, waiting for transfers between devices, local(): all_gather(v.astype(jnp.bfloat16), axis_name='dp').sum(axis=0)  341 us
    all_to_all x1, blocking collectives, exchange(): lax.all_to_all(rows, 'expert', split_axis=0, concat_axis=0, tiled=True)  65.8 us
    all_to_all x1, waiting for transfers between devices, exchange(): lax.all_to_all(rows, 'expert', split_axis=0, concat_axis=0, tiled=True)  21.1 us
    reduce_sum x3, other arithmetic, local(): all_gather(v.astype(jnp.bfloat16), axis_name='dp').sum(axis=0)  20.2 us
    all_to_all x1, starting transfers between devices, exchange(): lax.all_to_all(rows, 'expert', split_axis=0, concat_axis=0, tiled=True)  11.5 us
    dot_general x4, matrix products, contract_rows(): lax.dot_general(a, b, (((0,), (0,)), ((), ())), preferred_element_type=jn...  10.3 us
  transfers between devices with their start and end apart: 4, of which 4 were waited for; matrix products, arithmetic and copies ran while one was open for 5% of the time, Pallas kernels for 0%

profile of v1, /device:TPU:1, one launch (start us, length us, event | category | flops | bytes accessed | tf_op | source)
XLA Modules:
  0.0 512.5 jit_solution(8196883079974947065)
XLA Ops:
  10.2 1.7 convolution_convert_fusion
  12.1 65.8 %all_to_all.10 = bf16[64,16,1024]{2,1,0:T(8,128)(2,1)S(1)} all-to-all(bf16[64,16,1024]{2,1,0:T(8,128)(2,1)S(1)} %broadcast_select_fusion), channel_id=1, replica_groups=mesh['dp'=8,'expert'=64] {'expert'}, dimensions={0} | all-to-all | bytes 4194304 | tf_op jit(solution)/shard_map/all_to_all | solution.py:35
  78.0 1.5 reshape.52
  79.5 3.2 convolution_convert_fusion.1
  82.7 3.4 convolution_convert_fusion.2
  86.3 3.4 convolution_convert_fusion.3
  90.0 110.1 %all-gather.11.cloned.1.call-done = bf16[7168,768]{1,0:T(8,128)(2,1)} async-done(((bf16[896,768]{1,0:T(8,128)(2,1)}), bf16[7168,768]{1,0:T(8,128)(2,1)}) %all-gather.11.cloned.1.call-update) | async-done | bytes 11010064 | tf_op jit(solution)/shard_map/all_gather | solution.py:81
  200.1 6.5 %reduce_sum.85 = bf16[896,768]{1,0:T(8,128)(2,1)S(1)} reduce(bf16[8,896,768]{2,1,0:T(8,128)(2,1)} %bitcast.46, bf16[]{:T(256)} %constant.14.clone.1), dimensions={0}, to_apply=%region_5.6 | reduce | flops 4816896 | bytes 12386306 | tf_op jit(solution)/shard_map/reduce_sum | solution.py:81
  206.6 115.6 %all-gather.9.cloned.1.call-done = bf16[7168,768]{1,0:T(8,128)(2,1)} async-done(((bf16[896,768]{1,0:T(8,128)(2,1)}), bf16[7168,768]{1,0:T(8,128)(2,1)}) %all-gather.9.cloned.1.call-update) | async-done | bytes 11010064 | tf_op jit(solution)/shard_map/all_gather | solution.py:81
  322.2 7.2 %reduce_sum.84 = bf16[896,768]{1,0:T(8,128)(2,1)} reduce(bf16[8,896,768]{2,1,0:T(8,128)(2,1)} %bitcast.47, bf16[]{:T(256)} %constant.14.clone.1), dimensions={0}, to_apply=%region_4.5 | reduce | flops 4816896 | bytes 12386306 | tf_op jit(solution)/shard_map/reduce_sum | solution.py:81
  329.4 115.0 %all-gather.7.cloned.1.call-done = bf16[7168,768]{1,0:T(8,128)(2,1)} async-done(((bf16[896,768]{1,0:T(8,128)(2,1)}), bf16[7168,768]{1,0:T(8,128)(2,1)}) %all-gather.7.cloned.1.call-update) | async-done | bytes 11010064 | tf_op jit(solution)/shard_map/all_gather | solution.py:81
  444.3 6.5 %reduce_sum.83 = bf16[896,768]{1,0:T(8,128)(2,1)S(1)} reduce(bf16[8,896,768]{2,1,0:T(8,128)(2,1)} %bitcast.48, bf16[]{:T(256)} %constant.14.clone.1), dimensions={0}, to_apply=%region_3.4 | reduce | flops 4816896 | bytes 12386306 | tf_op jit(solution)/shard_map/reduce_sum | solution.py:81
  450.9 4.3 fusion.1
  455.2 1.1 copy-done.1
  457.1 0.9 fusion.24
  458.6 0.9 add_convert_fusion
  459.8 1.4 pad_maximum_fusion
  461.1 11.5 %all-to-all-start.1 = ((bf16[64,15,512]{2,1,0:T(8,128)(2,1)}), bf16[64,15,512]{2,1,0:T(8,128)(2,1)}, u32[]{:S(2)}, u32[]{:S(2)}) async-start(bf16[64,15,512]{2,1,0:T(8,128)(2,1)} %pad_maximum_fusion), calls=%async_computation.1 | async-start | bytes 2097152 | tf_op jit(solution)/shard_map/all_to_all | solution.py:35
  472.7 3.4 fusion.15
  476.0 1.9 fusion.14
  478.0 2.0 fusion.16
  480.0 21.1 %all-to-all-done.1 = bf16[64,15,512]{2,1,0:T(8,128)(2,1)} async-done(((bf16[64,15,512]{2,1,0:T(8,128)(2,1)}), bf16[64,15,512]{2,1,0:T(8,128)(2,1)}, u32[]{:S(2)}, u32[]{:S(2)}) %all-to-all-start.1) | async-done | bytes 983072 | tf_op jit(solution)/shard_map/all_to_all | solution.py:35
  501.1 0.9 slice_convert_fusion
  502.3 3.0 fusion.19
  (49 shorter events, 6.3 us)
Async XLA Ops:
  7.2 72.3 %copy-start = (bf16[1,512,768]{2,1,0:T(8,128)(2,1)S(1)}, bf16[1,512,768]{2,1,0:T(8,128)(2,1)}, u32[]{:S(2)}) copy-start(bf16[1,512,768]{2,1,0:T(8,128)(2,1)} %param.11) | copy-start | bytes 2359300
  7.2 192.9 %all-gather.11.cloned.1.call-start = ((), (), s32[]{:S(2)}) async-start(), calls=%async_computation.4 | async-start | bytes 12386304 | tf_op jit(solution)/shard_map/all_gather | solution.py:81
  8.8 3.0 copy-start.7
  82.6 239.6 %all-gather.9.cloned.1.call-start = ((), (), s32[]{:S(2)}) async-start(), calls=%async_computation.3 | async-start | bytes 12386304 | tf_op jit(solution)/shard_map/all_gather | solution.py:81
  86.1 358.2 %all-gather.7.cloned.1.call-start = ((), (), s32[]{:S(2)}) async-start(), calls=%async_computation.2 | async-start | bytes 12386304 | tf_op jit(solution)/shard_map/all_gather | solution.py:81
  455.2 1.1 copy-start.1
  455.2 1.8 copy-start.4
  457.0 1.3 copy-start.6
  457.0 1.5 copy-start.10
  461.1 11.5 %copy-start.3 = (bf16[896,1024]{1,0:T(8,128)(2,1)S(1)}, bf16[896,1024]{1,0:T(8,128)(2,1)}, u32[]{:S(2)}) copy-start(bf16[896,1024]{1,0:T(8,128)(2,1)} %reshape.52) | copy-start | bytes 5505028
  461.1 40.0 %all-to-all-start.1 = ((bf16[64,15,512]{2,1,0:T(8,128)(2,1)}), bf16[64,15,512]{2,1,0:T(8,128)(2,1)}, u32[]{:S(2)}, u32[]{:S(2)}) async-start(bf16[64,15,512]{2,1,0:T(8,128)(2,1)} %pad_maximum_fusion), calls=%async_computation.1 | async-start | bytes 2097152 | tf_op jit(solution)/shard_map/all_to_all | solution.py:35
  472.7 3.4 copy-start.5
  476.0 1.9 copy-start.2
  478.0 24.1 %copy-start.8 = (s32[64,128]{1,0:T(8,128)S(1)}, s32[64,128]{1,0:T(8,128)}, u32[]{:S(2)}) copy-start(s32[64,128]{1,0:T(8,128)} %copy-done.7) | copy-start | bytes 98308
  478.0 27.4 %copy-start.9 = (s32[128,6]{0,1:T(8,128)S(1)}, s32[128,6]{0,1:T(8,128)}, u32[]{:S(2)}) copy-start(s32[128,6]{0,1:T(8,128)} %param.9) | copy-start | bytes 9220
Sparse Core Ops, SparseCore 0:
  82.8 117.2 all-gather.10
  202.2 119.9 all-gather.8
  324.3 119.9 all-gather.6
